TPU v7x, 32 devices: a whole 2x2x4 slice. The times are simulated.
32 devices in a mesh: grp: 2 (over x), ta: 4 (over y, core), gz: 4 (over z).
Axes of the slice: x: 2, y: 2, z: 4, core: 2. Of those that a mesh axis runs over, the one named last changes fastest.
Arguments:
- coarse_links: bfloat16 [4, 4, 16, 9, 128, 128], P('ta', 'gz'), may hold values from -5 to 5
- right_sides: float32 [16, 4, 4, 16, 128], P(None, 'ta', 'gz', 'grp'), may hold values from -12 to 12
Outputs:
- solution: float32 [16, 4, 4, 16, 128], P(None, 'ta', 'gz', 'grp')
- residual: float32 [16, 4, 4, 16, 128], P(None, 'ta', 'gz', 'grp')
All inputs are finite; a program needn't handle non-finite values.
Results may differ from a plain program's by a relative error of at most 0.015.
The roundings to bfloat16 on the way count: a program that leaves them out, or rounds other values in their place, can miss the bound.
Values may be sent and summed in bfloat16 or wider, within the bound.
No kernel may reach another device: no remote copies, remote signals or barrier semaphores. Data moves between devices by JAX's collectives and lax.ppermute only.
A program may use at most 64 MiB of HBM per device.

v0:
```python
import jax
import jax.numpy as jnp
import numpy as np
from jax import lax
from jax.sharding import PartitionSpec as P

LX = 4
LY = 4
ITERS = 4


def extended(block, sides, width):
    for axis, dim in sides:
        count = lax.axis_size(axis)
        forward = [(i, i + 1) for i in range(count - 1)]
        forward.append((count - 1, 0))
        backward = [(target, source) for source, target in forward]
        low = lax.ppermute(
            lax.slice_in_dim(block, block.shape[dim] - width, None, axis=dim), axis, forward
        )
        high = lax.ppermute(lax.slice_in_dim(block, 0, width, axis=dim), axis, backward)
        block = jnp.concatenate([low, block, high], axis=dim)
    return block


def site_table():
    site_ids = np.arange(LX * LY)
    column = site_ids % LX
    row_of = site_ids // LX
    forward_x = row_of * LX + (column + 1) % LX
    backward_x = row_of * LX + (column - 1) % LX
    forward_y = (row_of + 1) % LY * LX + column
    backward_y = (row_of - 1) % LY * LX + column
    return np.stack([forward_x, backward_x, forward_y, backward_y], axis=1).astype(np.int32)


def hopping(link_part, centre, xy_plane, padded, table_part):
    extent = centre.shape
    planar = jnp.take(xy_plane, table_part.reshape(-1), axis=3).reshape(extent[:4] + (4, extent[4]))
    upper_z = padded[:, 1:-1, 2:]
    lower_z = padded[:, 1:-1, :-2]
    upper_t = padded[:, 2:, 1:-1]
    lower_t = padded[:, :-2, 1:-1]
    stacked = jnp.concatenate(
        [
            centre[:, :, :, :, None, :],
            planar,
            upper_z[:, :, :, :, None, :],
            lower_z[:, :, :, :, None, :],
            upper_t[:, :, :, :, None, :],
            lower_t[:, :, :, :, None, :],
        ],
        axis=4,
    )
    return jnp.einsum(
        "tzsmab,rtzsmb->rtzsa", link_part, stacked, preferred_element_type=jnp.float32
    )


def inner(left, right):
    return jnp.sum(left * right, axis=(1, 2, 3, 4))


def expand(values):
    return values.reshape(-1, 1, 1, 1, 1)


def solve(right_sides, apply_op, coeff_total, norm_total):
    solution = jnp.zeros_like(right_sides)
    residual = right_sides
    basis_q = []
    basis_p = []
    for iteration in range(ITERS):
        direction = residual.astype(jnp.bfloat16)
        mapped = apply_op(direction)
        search = direction.astype(jnp.float32)
        previous = len(basis_q)
        if previous > 0:
            coefficients = coeff_total(
                jnp.stack([inner(older, mapped) for older in basis_q], axis=1)
            )
        ortho_q = mapped
        ortho_p = search
        for position in range(previous):
            ortho_q = ortho_q - expand(coefficients[:, position]) * basis_q[position]
            ortho_p = ortho_p - expand(coefficients[:, position]) * basis_p[position]
        totals = norm_total(jnp.stack([inner(ortho_q, ortho_q), inner(ortho_q, residual)], axis=1))
        squared = totals[:, 0]
        projected = totals[:, 1]
        inverse = 1.0 / jnp.sqrt(squared)
        new_q = ortho_q * expand(inverse)
        new_p = ortho_p * expand(inverse)
        alpha = projected * inverse
        solution = solution + expand(alpha) * new_p
        residual = residual - expand(alpha) * new_q
        basis_q.append(new_q)
        basis_p.append(new_p)
    return (solution, residual)


def local(coarse_links, right_sides):
    full_table = jnp.asarray(site_table())
    site_count = right_sides.shape[3]
    offset = lax.axis_index("grp") * site_count
    link_part = lax.dynamic_slice_in_dim(coarse_links, offset, site_count, 2)
    table_part = lax.dynamic_slice_in_dim(full_table, offset, site_count, 0)

    def operate_sites(direction):
        xy_plane = lax.all_gather(direction, "grp", axis=3, tiled=True)
        padded = extended(direction, (("ta", 1), ("gz", 2)), 1)
        return hopping(link_part, direction, xy_plane, padded, table_part)

    def coeff_sites(values):
        return lax.psum(values, ("grp", "ta", "gz"))

    def norm_sites(values):
        return lax.psum(values, ("grp", "ta", "gz"))

    solution, residual = solve(right_sides, operate_sites, coeff_sites, norm_sites)
    return (solution, residual)


def solution(mesh):
    placed = (P("ta", "gz", None, None, None, None), P(None, "ta", "gz", "grp", None))
    return jax.shard_map(
        local,
        mesh=mesh,
        in_specs=placed,
        out_specs=(P(None, "ta", "gz", "grp", None), P(None, "ta", "gz", "grp", None)),
        check_vma=False,
    )
```

profile of v0, /device:TPU:0, one launch (start us, length us, event | category | flops | bytes accessed | tf_op | source)
XLA Modules:
  0.0 355.1 jit_solution(9772201396584370104)
XLA Ops:
  4.8 4.7 %all_gather.12 = bf16[16,1,1,16,128]{4,0,2,1,3:T(8,128)(2,1)S(1)} all-gather(bf16[16,1,1,8,128]{4,0,2,1,3:T(8,128)(2,1)S(1)} %bitcast.250), channel_id=1, replica_groups=mesh['grp'=2,'ta'=4,'gz'=4] {'grp'}, dimensions={3}, use_global_device_ids=true | all-gather | bytes 98304 | tf_op jit(solution)/shard_map/all_gather | solution.py:109
  10.2 3.7 %collective-permute-start.2 = (bf16[16,3,1,8,128]{4,0,3,2,1:T(8,128)(2,1)S(1)}, bf16[16,3,1,8,128]{4,0,3,2,1:T(8,128)(2,1)S(1)}, u32[]{:S(2)}, u32[]{:S(2)}) collective-permute-start(bf16[16,3,1,8,128]{4,0,3,2,1:T(8,128)(2,1)S(1)} %pad_maximum_fusion), channel_id=1, source_target_pairs={{1,0},{2,1},{3,2},{0,3},{5,4},{6,5},{7,6},{4,7},{9,8},{10,9},{11,1... | collective-permute-start | bytes 294920 | tf_op jit(solution)/shard_map/ppermute | solution.py:21
  14.0 3.1 collective-permute-done.2
  17.1 3.3 collective-permute-done.3
  20.4 2.6 multiply_reduce_fusion.13
  23.0 38.8 %psum.49 = f32[16,2]{0,1:T(2,128)S(1)} all-reduce(f32[16,2]{0,1:T(2,128)S(1)} %pad_maximum_fusion.5), channel_id=1, replica_groups=mesh['grp'=2,'ta'=4,'gz'=4] {'grp','ta','gz'}, use_global_device_ids=true, to_apply=%region_2.4 | all-reduce | flops 32 | bytes 256 | tf_op jit(solution)/shard_map/psum | solution.py:117
  63.3 4.8 %all_gather.13 = bf16[16,1,1,16,128]{4,0,2,1,3:T(8,128)(2,1)S(1)} all-gather(bf16[16,1,1,8,128]{4,0,2,1,3:T(8,128)(2,1)S(1)} %bitcast.251), channel_id=1, replica_groups=mesh['grp'=2,'ta'=4,'gz'=4] {'grp'}, dimensions={3}, use_global_device_ids=true | all-gather | bytes 98304 | tf_op jit(solution)/shard_map/all_gather | solution.py:109
  71.0 3.1 collective-permute-done.6
  74.2 3.2 collective-permute-done.7
  77.4 2.6 multiply_reduce_fusion.11
  80.0 38.6 %psum.50 = f32[16]{0:T(128)S(1)} all-reduce(f32[16]{0:T(128)S(1)} %get-tuple-element.42), channel_id=1, replica_groups=mesh['grp'=2,'ta'=4,'gz'=4] {'grp','ta','gz'}, use_global_device_ids=true, to_apply=%region_4.6 | all-reduce | flops 16 | bytes 128 | tf_op jit(solution)/shard_map/psum | solution.py:114
  118.8 40.8 %psum.51 = f32[16,2]{0,1:T(2,128)S(1)} all-reduce(f32[16,2]{0,1:T(2,128)S(1)} %pad_maximum_fusion.6), channel_id=1, replica_groups=mesh['grp'=2,'ta'=4,'gz'=4] {'grp','ta','gz'}, use_global_device_ids=true, to_apply=%region_7.9 | all-reduce | flops 32 | bytes 256 | tf_op jit(solution)/shard_map/psum | solution.py:117
  160.2 4.8 %all_gather.14 = bf16[16,1,1,16,128]{4,0,2,1,3:T(8,128)(2,1)S(1)} all-gather(bf16[16,1,1,8,128]{4,0,2,1,3:T(8,128)(2,1)S(1)} %bitcast.252), channel_id=1, replica_groups=mesh['grp'=2,'ta'=4,'gz'=4] {'grp'}, dimensions={3}, use_global_device_ids=true | all-gather | bytes 98304 | tf_op jit(solution)/shard_map/all_gather | solution.py:109
  167.9 3.1 collective-permute-done.10
  171.1 3.1 collective-permute-done.11
  174.2 2.6 multiply_reduce_fusion.8
  176.8 38.2 %psum.52 = f32[16,2]{0,1:T(2,128)S(1)} all-reduce(f32[16,2]{0,1:T(2,128)S(1)} %pad_maximum_fusion.7), channel_id=1, replica_groups=mesh['grp'=2,'ta'=4,'gz'=4] {'grp','ta','gz'}, use_global_device_ids=true, to_apply=%region_10.12 | all-reduce | flops 32 | bytes 256 | tf_op jit(solution)/shard_map/psum | solution.py:114
  215.3 41.4 %psum.53 = f32[16,2]{0,1:T(2,128)S(1)} all-reduce(f32[16,2]{0,1:T(2,128)S(1)} %pad_maximum_fusion.8), channel_id=1, replica_groups=mesh['grp'=2,'ta'=4,'gz'=4] {'grp','ta','gz'}, use_global_device_ids=true, to_apply=%region_13.15 | all-reduce | flops 32 | bytes 256 | tf_op jit(solution)/shard_map/psum | solution.py:117
  257.4 4.8 %all_gather.15 = bf16[16,1,1,16,128]{4,0,2,1,3:T(8,128)(2,1)S(1)} all-gather(bf16[16,1,1,8,128]{4,0,2,1,3:T(8,128)(2,1)S(1)} %bitcast.253), channel_id=1, replica_groups=mesh['grp'=2,'ta'=4,'gz'=4] {'grp'}, dimensions={3}, use_global_device_ids=true | all-gather | bytes 98304 | tf_op jit(solution)/shard_map/all_gather | solution.py:109
  265.1 3.1 collective-permute-done.14
  268.3 3.1 collective-permute-done.15
  271.4 2.6 multiply_reduce_fusion.4
  274.0 38.7 %psum.54 = f32[16,3]{0,1:T(4,128)S(1)} all-reduce(f32[16,3]{0,1:T(4,128)S(1)} %pad_maximum_fusion.4), channel_id=1, replica_groups=mesh['grp'=2,'ta'=4,'gz'=4] {'grp','ta','gz'}, use_global_device_ids=true, to_apply=%region_17.19 | all-reduce | flops 48 | bytes 384 | tf_op jit(solution)/shard_map/psum | solution.py:114
  313.0 40.6 %psum.55 = f32[16,2]{0,1:T(2,128)S(1)} all-reduce(f32[16,2]{0,1:T(2,128)S(1)} %pad_maximum_fusion.9), channel_id=1, replica_groups=mesh['grp'=2,'ta'=4,'gz'=4] {'grp','ta','gz'}, use_global_device_ids=true, to_apply=%region_20.22 | all-reduce | flops 32 | bytes 256 | tf_op jit(solution)/shard_map/psum | solution.py:117
  (87 shorter events, 18.7 us)
Async XLA Ops:
  1.5 8.7 %collective-permute-start.1 = (bf16[16,1,1,8,128]{4,0,3,2,1:T(8,128)(2,1)S(1)}, bf16[16,1,1,8,128]{4,0,3,2,1:T(8,128)(2,1)S(1)}, u32[]{:S(2)}, u32[]{:S(2)}) collective-permute-start(bf16[16,1,1,8,128]{4,0,3,2,1:T(8,128)(2,1)S(1)} %get-tuple-element.35), channel_id=1, source_target_pairs={{4,0},{8,4},{12,8},{0,12},{5,1},{9,5},{13,9},{1,13},{6,2},{10,6},{... | collective-permute-start | bytes 98312 | tf_op jit(solution)/shard_map/ppermute | solution.py:21
  4.0 6.2 %collective-permute-start = (bf16[16,1,1,8,128]{4,0,3,2,1:T(8,128)(2,1)S(1)}, bf16[16,1,1,8,128]{4,0,3,2,1:T(8,128)(2,1)S(1)}, u32[]{:S(2)}, u32[]{:S(2)}) collective-permute-start(bf16[16,1,1,8,128]{4,0,3,2,1:T(8,128)(2,1)S(1)} %get-tuple-element.35), channel_id=1, source_target_pairs={{0,4},{4,8},{8,12},{12,0},{1,5},{5,9},{9,13},{13,1},{2,6},{6,10},{... | collective-permute-start | bytes 98312 | tf_op jit(solution)/shard_map/ppermute | solution.py:18
  10.2 6.8 %collective-permute-start.2 = (bf16[16,3,1,8,128]{4,0,3,2,1:T(8,128)(2,1)S(1)}, bf16[16,3,1,8,128]{4,0,3,2,1:T(8,128)(2,1)S(1)}, u32[]{:S(2)}, u32[]{:S(2)}) collective-permute-start(bf16[16,3,1,8,128]{4,0,3,2,1:T(8,128)(2,1)S(1)} %pad_maximum_fusion), channel_id=1, source_target_pairs={{1,0},{2,1},{3,2},{0,3},{5,4},{6,5},{7,6},{4,7},{9,8},{10,9},{11,1... | collective-permute-start | bytes 294920 | tf_op jit(solution)/shard_map/ppermute | solution.py:21
  13.9 6.5 %collective-permute-start.3 = (bf16[16,3,1,8,128]{4,0,3,2,1:T(8,128)(2,1)S(1)}, bf16[16,3,1,8,128]{4,0,3,2,1:T(8,128)(2,1)S(1)}, u32[]{:S(2)}, u32[]{:S(2)}) collective-permute-start(bf16[16,3,1,8,128]{4,0,3,2,1:T(8,128)(2,1)S(1)} %pad_maximum_fusion), channel_id=1, source_target_pairs={{0,1},{1,2},{2,3},{3,0},{4,5},{5,6},{6,7},{7,4},{8,9},{9,10},{10,1... | collective-permute-start | bytes 294920 | tf_op jit(solution)/shard_map/ppermute | solution.py:18
  62.8 6.1 %collective-permute-start.5 = (bf16[16,1,1,8,128]{4,0,3,2,1:T(8,128)(2,1)S(1)}, bf16[16,1,1,8,128]{4,0,3,2,1:T(8,128)(2,1)S(1)}, u32[]{:S(2)}, u32[]{:S(2)}) collective-permute-start(bf16[16,1,1,8,128]{4,0,3,2,1:T(8,128)(2,1)S(1)} %get-tuple-element.32), channel_id=1, source_target_pairs={{4,0},{8,4},{12,8},{0,12},{5,1},{9,5},{13,9},{1,13},{6,2},{10,6},{... | collective-permute-start | bytes 98312 | tf_op jit(solution)/shard_map/ppermute | solution.py:21
  62.9 6.0 %collective-permute-start.4 = (bf16[16,1,1,8,128]{4,0,3,2,1:T(8,128)(2,1)S(1)}, bf16[16,1,1,8,128]{4,0,3,2,1:T(8,128)(2,1)S(1)}, u32[]{:S(2)}, u32[]{:S(2)}) collective-permute-start(bf16[16,1,1,8,128]{4,0,3,2,1:T(8,128)(2,1)S(1)} %get-tuple-element.32), channel_id=1, source_target_pairs={{0,4},{4,8},{8,12},{12,0},{1,5},{5,9},{9,13},{13,1},{2,6},{6,10},{... | collective-permute-start | bytes 98312 | tf_op jit(solution)/shard_map/ppermute | solution.py:18
  68.9 5.3 %collective-permute-start.6 = (bf16[16,3,1,8,128]{4,0,3,2,1:T(8,128)(2,1)S(1)}, bf16[16,3,1,8,128]{4,0,3,2,1:T(8,128)(2,1)S(1)}, u32[]{:S(2)}, u32[]{:S(2)}) collective-permute-start(bf16[16,3,1,8,128]{4,0,3,2,1:T(8,128)(2,1)S(1)} %pad_maximum_fusion.1), channel_id=1, source_target_pairs={{1,0},{2,1},{3,2},{0,3},{5,4},{6,5},{7,6},{4,7},{9,8},{10,9},{11,1... | collective-permute-start | bytes 294920 | tf_op jit(solution)/shard_map/ppermute | solution.py:21
  70.6 6.8 %collective-permute-start.7 = (bf16[16,3,1,8,128]{4,0,3,2,1:T(8,128)(2,1)S(1)}, bf16[16,3,1,8,128]{4,0,3,2,1:T(8,128)(2,1)S(1)}, u32[]{:S(2)}, u32[]{:S(2)}) collective-permute-start(bf16[16,3,1,8,128]{4,0,3,2,1:T(8,128)(2,1)S(1)} %pad_maximum_fusion.1), channel_id=1, source_target_pairs={{0,1},{1,2},{2,3},{3,0},{4,5},{5,6},{6,7},{7,4},{8,9},{9,10},{10,1... | collective-permute-start | bytes 294920 | tf_op jit(solution)/shard_map/ppermute | solution.py:18
  159.7 6.1 %collective-permute-start.9 = (bf16[16,1,1,8,128]{4,0,3,2,1:T(8,128)(2,1)S(1)}, bf16[16,1,1,8,128]{4,0,3,2,1:T(8,128)(2,1)S(1)}, u32[]{:S(2)}, u32[]{:S(2)}) collective-permute-start(bf16[16,1,1,8,128]{4,0,3,2,1:T(8,128)(2,1)S(1)} %get-tuple-element.28), channel_id=1, source_target_pairs={{4,0},{8,4},{12,8},{0,12},{5,1},{9,5},{13,9},{1,13},{6,2},{10,6},{... | collective-permute-start | bytes 98312 | tf_op jit(solution)/shard_map/ppermute | solution.py:21
  160.0 5.8 %collective-permute-start.8 = (bf16[16,1,1,8,128]{4,0,3,2,1:T(8,128)(2,1)S(1)}, bf16[16,1,1,8,128]{4,0,3,2,1:T(8,128)(2,1)S(1)}, u32[]{:S(2)}, u32[]{:S(2)}) collective-permute-start(bf16[16,1,1,8,128]{4,0,3,2,1:T(8,128)(2,1)S(1)} %get-tuple-element.28), channel_id=1, source_target_pairs={{0,4},{4,8},{8,12},{12,0},{1,5},{5,9},{9,13},{13,1},{2,6},{6,10},{... | collective-permute-start | bytes 98312 | tf_op jit(solution)/shard_map/ppermute | solution.py:18
  165.8 5.3 %collective-permute-start.10 = (bf16[16,3,1,8,128]{4,0,3,2,1:T(8,128)(2,1)S(1)}, bf16[16,3,1,8,128]{4,0,3,2,1:T(8,128)(2,1)S(1)}, u32[]{:S(2)}, u32[]{:S(2)}) collective-permute-start(bf16[16,3,1,8,128]{4,0,3,2,1:T(8,128)(2,1)S(1)} %pad_maximum_fusion.2), channel_id=1, source_target_pairs={{1,0},{2,1},{3,2},{0,3},{5,4},{6,5},{7,6},{4,7},{9,8},{10,9},{11,1... | collective-permute-start | bytes 294920 | tf_op jit(solution)/shard_map/ppermute | solution.py:21
  167.4 6.8 %collective-permute-start.11 = (bf16[16,3,1,8,128]{4,0,3,2,1:T(8,128)(2,1)S(1)}, bf16[16,3,1,8,128]{4,0,3,2,1:T(8,128)(2,1)S(1)}, u32[]{:S(2)}, u32[]{:S(2)}) collective-permute-start(bf16[16,3,1,8,128]{4,0,3,2,1:T(8,128)(2,1)S(1)} %pad_maximum_fusion.2), channel_id=1, source_target_pairs={{0,1},{1,2},{2,3},{3,0},{4,5},{5,6},{6,7},{7,4},{8,9},{9,10},{10,1... | collective-permute-start | bytes 294920 | tf_op jit(solution)/shard_map/ppermute | solution.py:18
  256.8 6.1 %collective-permute-start.13 = (bf16[16,1,1,8,128]{4,0,3,2,1:T(8,128)(2,1)S(1)}, bf16[16,1,1,8,128]{4,0,3,2,1:T(8,128)(2,1)S(1)}, u32[]{:S(2)}, u32[]{:S(2)}) collective-permute-start(bf16[16,1,1,8,128]{4,0,3,2,1:T(8,128)(2,1)S(1)} %get-tuple-element.24), channel_id=1, source_target_pairs={{4,0},{8,4},{12,8},{0,12},{5,1},{9,5},{13,9},{1,13},{6,2},{10,6},{... | collective-permute-start | bytes 98312 | tf_op jit(solution)/shard_map/ppermute | solution.py:21
  257.1 5.8 %collective-permute-start.12 = (bf16[16,1,1,8,128]{4,0,3,2,1:T(8,128)(2,1)S(1)}, bf16[16,1,1,8,128]{4,0,3,2,1:T(8,128)(2,1)S(1)}, u32[]{:S(2)}, u32[]{:S(2)}) collective-permute-start(bf16[16,1,1,8,128]{4,0,3,2,1:T(8,128)(2,1)S(1)} %get-tuple-element.24), channel_id=1, source_target_pairs={{0,4},{4,8},{8,12},{12,0},{1,5},{5,9},{9,13},{13,1},{2,6},{6,10},{... | collective-permute-start | bytes 98312 | tf_op jit(solution)/shard_map/ppermute | solution.py:18
  263.0 5.3 %collective-permute-start.14 = (bf16[16,3,1,8,128]{4,0,3,2,1:T(8,128)(2,1)S(1)}, bf16[16,3,1,8,128]{4,0,3,2,1:T(8,128)(2,1)S(1)}, u32[]{:S(2)}, u32[]{:S(2)}) collective-permute-start(bf16[16,3,1,8,128]{4,0,3,2,1:T(8,128)(2,1)S(1)} %pad_maximum_fusion.3), channel_id=1, source_target_pairs={{1,0},{2,1},{3,2},{0,3},{5,4},{6,5},{7,6},{4,7},{9,8},{10,9},{11,1... | collective-permute-start | bytes 294920 | tf_op jit(solution)/shard_map/ppermute | solution.py:21
  264.5 6.8 %collective-permute-start.15 = (bf16[16,3,1,8,128]{4,0,3,2,1:T(8,128)(2,1)S(1)}, bf16[16,3,1,8,128]{4,0,3,2,1:T(8,128)(2,1)S(1)}, u32[]{:S(2)}, u32[]{:S(2)}) collective-permute-start(bf16[16,3,1,8,128]{4,0,3,2,1:T(8,128)(2,1)S(1)} %pad_maximum_fusion.3), channel_id=1, source_target_pairs={{0,1},{1,2},{2,3},{3,0},{4,5},{5,6},{6,7},{7,4},{8,9},{9,10},{10,1... | collective-permute-start | bytes 294920 | tf_op jit(solution)/shard_map/ppermute | solution.py:18
where the time goes:
time: 356 us; the launch traced here: 355 us
  blocking collectives  296 us (83%)
  waiting for transfers between devices  25.2 us (7%)
  starting transfers between devices  14.3 us (4%)
  matrix products  10.3 us (3%)
  local copies, waits for them, and re-layouts  5.53 us (2%)
    psum x4, blocking collectives, norm_sites(): return lax.psum(values, ('grp', 'ta', 'gz'))  162 us
    psum x3, blocking collectives, coeff_sites(): return lax.psum(values, ('grp', 'ta', 'gz'))  116 us
    all_gather x4, blocking collectives, operate_sites(): xy_plane = lax.all_gather(direction, 'grp', axis=3, tiled=True)  19.1 us
    ppermute x8, waiting for transfers between devices, extended(): lax.ppermute(lax.slice_in_dim(block, block.shape[dim] - width, None, axis...  12.7 us
    ppermute x8, waiting for transfers between devices, extended(): lax.ppermute(lax.slice_in_dim(block, 0, width, axis=dim), axis, backward)  12.6 us
    ppermute x8, starting transfers between devices, extended(): lax.ppermute(lax.slice_in_dim(block, 0, width, axis=dim), axis, backward)  11.6 us
    dot_general x4, matrix products, hopping(): jnp.einsum('tzsmab,rtzsmb->rtzsa', link_part, stacked, preferred_element_...  10.3 us
  transfers between devices with their start and end apart: 16, of which 8 were waited for; matrix products, arithmetic and copies ran while one was open for 1% of the time, Pallas kernels for 0%

commit v1 on v0

--- a/solution.py
+++ b/solution.py
@@ -114,7 +114,7 @@
         return lax.psum(values, ("grp", "ta", "gz"))
 
     def norm_sites(values):
-        return lax.psum(values, ("grp", "ta", "gz"))
+        return jnp.sum(lax.all_gather(values, ("grp", "ta", "gz")), axis=0)
 
     solution, residual = solve(right_sides, operate_sites, coeff_sites, norm_sites)
     return (solution, residual)

time: 356 us -> 448 us (1.26)
  blocking collectives: 296 us -> 393 us
  waiting for transfers between devices: 25.2 us -> 20.2 us
    all_gather x0 -> x4, blocking collectives: none -> 262 us  [norm_sites(): return jnp.sum(lax.all_gather(values, ('grp', 'ta', 'gz')), axis=0)]
    psum x4 -> x0, blocking collectives: 162 us -> none  [norm_sites(): return lax.psum(values, ('grp', 'ta', 'gz'))]
    ppermute x8, waiting for transfers between devices: 12.7 us -> 5.61 us  [extended(): lax.ppermute(lax.slice_in_dim(block, block.shape[dim] - width, None, axis...]
    ppermute x8, starting transfers between devices: 11.6 us -> 6.9 us  [extended(): lax.ppermute(lax.slice_in_dim(block, 0, width, axis=dim), axis, backward)]
    ppermute x8, starting transfers between devices: 2.67 us -> 7.35 us  [extended(): lax.ppermute(lax.slice_in_dim(block, block.shape[dim] - width, None, axis...]
  transfers between devices with their start and end apart: 16 -> 16, of which waited for: 8 -> 7; matrix products, arithmetic and copies ran while one was open for 1% -> 1% of each run, Pallas kernels for 0% -> 0%
where the time goes in v1:
time: 448 us; the launch traced here: 447 us
  blocking collectives  393 us (88%)
  waiting for transfers between devices  20.2 us (5%)
  starting transfers between devices  14.2 us (3%)
  matrix products  10.3 us (2%)
  local copies, waits for them, and re-layouts  5.55 us (1%)
    all_gather x4, blocking collectives, norm_sites(): return jnp.sum(lax.all_gather(values, ('grp', 'ta', 'gz')), axis=0)  262 us
    psum x3, blocking collectives, coeff_sites(): return lax.psum(values, ('grp', 'ta', 'gz'))  113 us
    all_gather x4, blocking collectives, operate_sites(): xy_plane = lax.all_gather(direction, 'grp', axis=3, tiled=True)  18.4 us
    ppermute x8, waiting for transfers between devices, extended(): lax.ppermute(lax.slice_in_dim(block, 0, width, axis=dim), axis, backward)  14.6 us
    dot_general x4, matrix products, hopping(): jnp.einsum('tzsmab,rtzsmb->rtzsa', link_part, stacked, preferred_element_...  10.3 us
  transfers between devices with their start and end apart: 16, of which 7 were waited for; matrix products, arithmetic and copies ran while one was open for 1% of the time, Pallas kernels for 0%

profile of v1, /device:TPU:0, one launch (start us, length us, event | category | flops | bytes accessed | tf_op | source)
XLA Modules:
  0.0 447.5 jit_solution(15727426360550305694)
XLA Ops:
  1.5 2.5 collective-permute-start.1
  4.8 4.7 %all_gather.36 = bf16[16,1,1,16,128]{4,0,2,1,3:T(8,128)(2,1)S(1)} all-gather(bf16[16,1,1,8,128]{4,0,2,1,3:T(8,128)(2,1)S(1)} %bitcast.258), channel_id=1, replica_groups=mesh['grp'=2,'ta'=4,'gz'=4] {'grp'}, dimensions={3}, use_global_device_ids=true | all-gather | bytes 98304 | tf_op jit(solution)/shard_map/all_gather | solution.py:109
  10.2 3.7 collective-permute-start.2
  14.0 3.1 collective-permute-done.2
  17.1 3.3 collective-permute-done.3
  20.4 2.6 multiply_reduce_fusion.13
  23.0 64.2 %all-gather.4 = f32[32,16,2]{1,2,0:T(2,128)S(1)} all-gather(f32[1,16,2]{1,2,0:T(2,128)S(1)} %maximum_bitcast_fusion), channel_id=2, replica_groups=mesh['grp'=2,'ta'=4,'gz'=4] {'grp','ta','gz'}, dimensions={0}, use_global_device_ids=true | all-gather | bytes 4224 | tf_op jit(solution)/shard_map/all_gather | solution.py:117
  88.7 4.6 %all_gather.39 = bf16[16,1,1,16,128]{4,0,2,1,3:T(8,128)(2,1)S(1)} all-gather(bf16[16,1,1,8,128]{4,0,2,1,3:T(8,128)(2,1)S(1)} %bitcast.259), channel_id=1, replica_groups=mesh['grp'=2,'ta'=4,'gz'=4] {'grp'}, dimensions={3}, use_global_device_ids=true | all-gather | bytes 98304 | tf_op jit(solution)/shard_map/all_gather | solution.py:109
  96.2 3.4 collective-permute-done.6
  100.9 2.6 multiply_reduce_fusion.11
  103.5 37.9 %psum.21 = f32[16]{0:T(128)S(1)} all-reduce(f32[16]{0:T(128)S(1)} %get-tuple-element.42), channel_id=1, replica_groups=mesh['grp'=2,'ta'=4,'gz'=4] {'grp','ta','gz'}, use_global_device_ids=true, to_apply=%region_4.6 | all-reduce | flops 16 | bytes 128 | tf_op jit(solution)/shard_map/psum | solution.py:114
  141.6 66.1 %all-gather.5 = f32[32,16,2]{1,2,0:T(2,128)S(1)} all-gather(f32[1,16,2]{1,2,0:T(2,128)S(1)} %maximum_bitcast_fusion.1), channel_id=3, replica_groups=mesh['grp'=2,'ta'=4,'gz'=4] {'grp','ta','gz'}, dimensions={0}, use_global_device_ids=true | all-gather | bytes 4224 | tf_op jit(solution)/shard_map/all_gather | solution.py:117
  208.5 4.6 %all_gather.42 = bf16[16,1,1,16,128]{4,0,2,1,3:T(8,128)(2,1)S(1)} all-gather(bf16[16,1,1,8,128]{4,0,2,1,3:T(8,128)(2,1)S(1)} %bitcast.260), channel_id=1, replica_groups=mesh['grp'=2,'ta'=4,'gz'=4] {'grp'}, dimensions={3}, use_global_device_ids=true | all-gather | bytes 98304 | tf_op jit(solution)/shard_map/all_gather | solution.py:109
  213.9 2.1 collective-permute-start.11
  215.9 3.5 collective-permute-done.10
  220.4 2.6 multiply_reduce_fusion.8
  223.0 37.8 %psum.22 = f32[16,2]{0,1:T(2,128)S(1)} all-reduce(f32[16,2]{0,1:T(2,128)S(1)} %pad_maximum_fusion.5), channel_id=1, replica_groups=mesh['grp'=2,'ta'=4,'gz'=4] {'grp','ta','gz'}, use_global_device_ids=true, to_apply=%region_10.12 | all-reduce | flops 32 | bytes 256 | tf_op jit(solution)/shard_map/psum | solution.py:114
  261.1 65.7 %all-gather.6 = f32[32,16,2]{1,2,0:T(2,128)S(1)} all-gather(f32[1,16,2]{1,2,0:T(2,128)S(1)} %maximum_bitcast_fusion.2), channel_id=4, replica_groups=mesh['grp'=2,'ta'=4,'gz'=4] {'grp','ta','gz'}, dimensions={0}, use_global_device_ids=true | all-gather | bytes 4224 | tf_op jit(solution)/shard_map/all_gather | solution.py:117
  327.5 4.6 %all_gather.45 = bf16[16,1,1,16,128]{4,0,2,1,3:T(8,128)(2,1)S(1)} all-gather(bf16[16,1,1,8,128]{4,0,2,1,3:T(8,128)(2,1)S(1)} %bitcast.261), channel_id=1, replica_groups=mesh['grp'=2,'ta'=4,'gz'=4] {'grp'}, dimensions={3}, use_global_device_ids=true | all-gather | bytes 98304 | tf_op jit(solution)/shard_map/all_gather | solution.py:109
  333.0 2.0 collective-permute-start.15
  335.0 4.6 %collective-permute-done.14 = bf16[16,3,1,8,128]{4,0,3,2,1:T(8,128)(2,1)S(1)} collective-permute-done((bf16[16,3,1,8,128]{4,0,3,2,1:T(8,128)(2,1)S(1)}, bf16[16,3,1,8,128]{4,0,3,2,1:T(8,128)(2,1)S(1)}, u32[]{:S(2)}, u32[]{:S(2)}) %collective-permute-start.14) | collective-permute-done | bytes 98336 | tf_op jit(solution)/shard_map/ppermute | solution.py:21
  339.6 2.6 multiply_reduce_fusion.4
  342.3 37.8 %psum.23 = f32[16,3]{0,1:T(4,128)S(1)} all-reduce(f32[16,3]{0,1:T(4,128)S(1)} %pad_maximum_fusion.4), channel_id=1, replica_groups=mesh['grp'=2,'ta'=4,'gz'=4] {'grp','ta','gz'}, use_global_device_ids=true, to_apply=%region_17.19 | all-reduce | flops 48 | bytes 384 | tf_op jit(solution)/shard_map/psum | solution.py:114
  380.3 65.6 %all-gather.7 = f32[32,16,2]{1,2,0:T(2,128)S(1)} all-gather(f32[1,16,2]{1,2,0:T(2,128)S(1)} %maximum_bitcast_fusion.3), channel_id=5, replica_groups=mesh['grp'=2,'ta'=4,'gz'=4] {'grp','ta','gz'}, dimensions={0}, use_global_device_ids=true | all-gather | bytes 4224 | tf_op jit(solution)/shard_map/all_gather | solution.py:117
  (91 shorter events, 14.6 us)
Async XLA Ops:
  1.5 8.7 %collective-permute-start.1 = (bf16[16,1,1,8,128]{4,0,3,2,1:T(8,128)(2,1)S(1)}, bf16[16,1,1,8,128]{4,0,3,2,1:T(8,128)(2,1)S(1)}, u32[]{:S(2)}, u32[]{:S(2)}) collective-permute-start(bf16[16,1,1,8,128]{4,0,3,2,1:T(8,128)(2,1)S(1)} %get-tuple-element.35), channel_id=1, source_target_pairs={{4,0},{8,4},{12,8},{0,12},{5,1},{9,5},{13,9},{1,13},{6,2},{10,6},{... | collective-permute-start | bytes 98312 | tf_op jit(solution)/shard_map/ppermute | solution.py:21
  4.0 6.2 %collective-permute-start = (bf16[16,1,1,8,128]{4,0,3,2,1:T(8,128)(2,1)S(1)}, bf16[16,1,1,8,128]{4,0,3,2,1:T(8,128)(2,1)S(1)}, u32[]{:S(2)}, u32[]{:S(2)}) collective-permute-start(bf16[16,1,1,8,128]{4,0,3,2,1:T(8,128)(2,1)S(1)} %get-tuple-element.35), channel_id=1, source_target_pairs={{0,4},{4,8},{8,12},{12,0},{1,5},{5,9},{9,13},{13,1},{2,6},{6,10},{... | collective-permute-start | bytes 98312 | tf_op jit(solution)/shard_map/ppermute | solution.py:18
  10.2 6.8 %collective-permute-start.2 = (bf16[16,3,1,8,128]{4,0,3,2,1:T(8,128)(2,1)S(1)}, bf16[16,3,1,8,128]{4,0,3,2,1:T(8,128)(2,1)S(1)}, u32[]{:S(2)}, u32[]{:S(2)}) collective-permute-start(bf16[16,3,1,8,128]{4,0,3,2,1:T(8,128)(2,1)S(1)} %pad_maximum_fusion), channel_id=1, source_target_pairs={{1,0},{2,1},{3,2},{0,3},{5,4},{6,5},{7,6},{4,7},{9,8},{10,9},{11,1... | collective-permute-start | bytes 294920 | tf_op jit(solution)/shard_map/ppermute | solution.py:21
  13.9 6.5 %collective-permute-start.3 = (bf16[16,3,1,8,128]{4,0,3,2,1:T(8,128)(2,1)S(1)}, bf16[16,3,1,8,128]{4,0,3,2,1:T(8,128)(2,1)S(1)}, u32[]{:S(2)}, u32[]{:S(2)}) collective-permute-start(bf16[16,3,1,8,128]{4,0,3,2,1:T(8,128)(2,1)S(1)} %pad_maximum_fusion), channel_id=1, source_target_pairs={{0,1},{1,2},{2,3},{3,0},{4,5},{5,6},{6,7},{7,4},{8,9},{9,10},{10,1... | collective-permute-start | bytes 294920 | tf_op jit(solution)/shard_map/ppermute | solution.py:18
  88.1 5.8 %collective-permute-start.5 = (bf16[16,1,1,8,128]{4,0,3,2,1:T(8,128)(2,1)S(1)}, bf16[16,1,1,8,128]{4,0,3,2,1:T(8,128)(2,1)S(1)}, u32[]{:S(2)}, u32[]{:S(2)}) collective-permute-start(bf16[16,1,1,8,128]{4,0,3,2,1:T(8,128)(2,1)S(1)} %get-tuple-element.32), channel_id=1, source_target_pairs={{4,0},{8,4},{12,8},{0,12},{5,1},{9,5},{13,9},{1,13},{6,2},{10,6},{... | collective-permute-start | bytes 98312 | tf_op jit(solution)/shard_map/ppermute | solution.py:21
  88.2 5.8 %collective-permute-start.4 = (bf16[16,1,1,8,128]{4,0,3,2,1:T(8,128)(2,1)S(1)}, bf16[16,1,1,8,128]{4,0,3,2,1:T(8,128)(2,1)S(1)}, u32[]{:S(2)}, u32[]{:S(2)}) collective-permute-start(bf16[16,1,1,8,128]{4,0,3,2,1:T(8,128)(2,1)S(1)} %get-tuple-element.32), channel_id=1, source_target_pairs={{0,4},{4,8},{8,12},{12,0},{1,5},{5,9},{9,13},{13,1},{2,6},{6,10},{... | collective-permute-start | bytes 98312 | tf_op jit(solution)/shard_map/ppermute | solution.py:18
  94.0 5.6 %collective-permute-start.6 = (bf16[16,3,1,8,128]{4,0,3,2,1:T(8,128)(2,1)S(1)}, bf16[16,3,1,8,128]{4,0,3,2,1:T(8,128)(2,1)S(1)}, u32[]{:S(2)}, u32[]{:S(2)}) collective-permute-start(bf16[16,3,1,8,128]{4,0,3,2,1:T(8,128)(2,1)S(1)} %pad_maximum_fusion.1), channel_id=1, source_target_pairs={{1,0},{2,1},{3,2},{0,3},{5,4},{6,5},{7,6},{4,7},{9,8},{10,9},{11,1... | collective-permute-start | bytes 294920 | tf_op jit(solution)/shard_map/ppermute | solution.py:21
  94.4 6.5 %collective-permute-start.7 = (bf16[16,3,1,8,128]{4,0,3,2,1:T(8,128)(2,1)S(1)}, bf16[16,3,1,8,128]{4,0,3,2,1:T(8,128)(2,1)S(1)}, u32[]{:S(2)}, u32[]{:S(2)}) collective-permute-start(bf16[16,3,1,8,128]{4,0,3,2,1:T(8,128)(2,1)S(1)} %pad_maximum_fusion.1), channel_id=1, source_target_pairs={{0,1},{1,2},{2,3},{3,0},{4,5},{5,6},{6,7},{7,4},{8,9},{9,10},{10,1... | collective-permute-start | bytes 294920 | tf_op jit(solution)/shard_map/ppermute | solution.py:18
  207.9 5.8 %collective-permute-start.9 = (bf16[16,1,1,8,128]{4,0,3,2,1:T(8,128)(2,1)S(1)}, bf16[16,1,1,8,128]{4,0,3,2,1:T(8,128)(2,1)S(1)}, u32[]{:S(2)}, u32[]{:S(2)}) collective-permute-start(bf16[16,1,1,8,128]{4,0,3,2,1:T(8,128)(2,1)S(1)} %get-tuple-element.28), channel_id=1, source_target_pairs={{4,0},{8,4},{12,8},{0,12},{5,1},{9,5},{13,9},{1,13},{6,2},{10,6},{... | collective-permute-start | bytes 98312 | tf_op jit(solution)/shard_map/ppermute | solution.py:21
  208.0 5.8 %collective-permute-start.8 = (bf16[16,1,1,8,128]{4,0,3,2,1:T(8,128)(2,1)S(1)}, bf16[16,1,1,8,128]{4,0,3,2,1:T(8,128)(2,1)S(1)}, u32[]{:S(2)}, u32[]{:S(2)}) collective-permute-start(bf16[16,1,1,8,128]{4,0,3,2,1:T(8,128)(2,1)S(1)} %get-tuple-element.28), channel_id=1, source_target_pairs={{0,4},{4,8},{8,12},{12,0},{1,5},{5,9},{9,13},{13,1},{2,6},{6,10},{... | collective-permute-start | bytes 98312 | tf_op jit(solution)/shard_map/ppermute | solution.py:18
  213.8 5.6 %collective-permute-start.10 = (bf16[16,3,1,8,128]{4,0,3,2,1:T(8,128)(2,1)S(1)}, bf16[16,3,1,8,128]{4,0,3,2,1:T(8,128)(2,1)S(1)}, u32[]{:S(2)}, u32[]{:S(2)}) collective-permute-start(bf16[16,3,1,8,128]{4,0,3,2,1:T(8,128)(2,1)S(1)} %pad_maximum_fusion.2), channel_id=1, source_target_pairs={{1,0},{2,1},{3,2},{0,3},{5,4},{6,5},{7,6},{4,7},{9,8},{10,9},{11,1... | collective-permute-start | bytes 294920 | tf_op jit(solution)/shard_map/ppermute | solution.py:21
  213.9 6.6 %collective-permute-start.11 = (bf16[16,3,1,8,128]{4,0,3,2,1:T(8,128)(2,1)S(1)}, bf16[16,3,1,8,128]{4,0,3,2,1:T(8,128)(2,1)S(1)}, u32[]{:S(2)}, u32[]{:S(2)}) collective-permute-start(bf16[16,3,1,8,128]{4,0,3,2,1:T(8,128)(2,1)S(1)} %pad_maximum_fusion.2), channel_id=1, source_target_pairs={{0,1},{1,2},{2,3},{3,0},{4,5},{5,6},{6,7},{7,4},{8,9},{9,10},{10,1... | collective-permute-start | bytes 294920 | tf_op jit(solution)/shard_map/ppermute | solution.py:18
  326.9 5.8 %collective-permute-start.13 = (bf16[16,1,1,8,128]{4,0,3,2,1:T(8,128)(2,1)S(1)}, bf16[16,1,1,8,128]{4,0,3,2,1:T(8,128)(2,1)S(1)}, u32[]{:S(2)}, u32[]{:S(2)}) collective-permute-start(bf16[16,1,1,8,128]{4,0,3,2,1:T(8,128)(2,1)S(1)} %get-tuple-element.24), channel_id=1, source_target_pairs={{4,0},{8,4},{12,8},{0,12},{5,1},{9,5},{13,9},{1,13},{6,2},{10,6},{... | collective-permute-start | bytes 98312 | tf_op jit(solution)/shard_map/ppermute | solution.py:21
  327.0 5.8 %collective-permute-start.12 = (bf16[16,1,1,8,128]{4,0,3,2,1:T(8,128)(2,1)S(1)}, bf16[16,1,1,8,128]{4,0,3,2,1:T(8,128)(2,1)S(1)}, u32[]{:S(2)}, u32[]{:S(2)}) collective-permute-start(bf16[16,1,1,8,128]{4,0,3,2,1:T(8,128)(2,1)S(1)} %get-tuple-element.24), channel_id=1, source_target_pairs={{0,4},{4,8},{8,12},{12,0},{1,5},{5,9},{9,13},{13,1},{2,6},{6,10},{... | collective-permute-start | bytes 98312 | tf_op jit(solution)/shard_map/ppermute | solution.py:18
  332.8 6.8 %collective-permute-start.14 = (bf16[16,3,1,8,128]{4,0,3,2,1:T(8,128)(2,1)S(1)}, bf16[16,3,1,8,128]{4,0,3,2,1:T(8,128)(2,1)S(1)}, u32[]{:S(2)}, u32[]{:S(2)}) collective-permute-start(bf16[16,3,1,8,128]{4,0,3,2,1:T(8,128)(2,1)S(1)} %pad_maximum_fusion.3), channel_id=1, source_target_pairs={{1,0},{2,1},{3,2},{0,3},{5,4},{6,5},{7,6},{4,7},{9,8},{10,9},{11,1... | collective-permute-start | bytes 294920 | tf_op jit(solution)/shard_map/ppermute | solution.py:21
  333.0 6.6 %collective-permute-start.15 = (bf16[16,3,1,8,128]{4,0,3,2,1:T(8,128)(2,1)S(1)}, bf16[16,3,1,8,128]{4,0,3,2,1:T(8,128)(2,1)S(1)}, u32[]{:S(2)}, u32[]{:S(2)}) collective-permute-start(bf16[16,3,1,8,128]{4,0,3,2,1:T(8,128)(2,1)S(1)} %pad_maximum_fusion.3), channel_id=1, source_target_pairs={{0,1},{1,2},{2,3},{3,0},{4,5},{5,6},{6,7},{7,4},{8,9},{9,10},{10,1... | collective-permute-start | bytes 294920 | tf_op jit(solution)/shard_map/ppermute | solution.py:18
